TPU v7x, 32 devices: a whole 2x2x4 slice. The times are simulated.
32 devices in a mesh: tm: 2 (over x), vox: 8 (over z, y), feat: 2 (over core).
Axes of the slice: x: 2, y: 2, z: 4, core: 2. Of those that a mesh axis runs over, the one named last changes fastest.
Arguments:
- design_matrix: bfloat16 [256, 4096], P(None, ('tm', 'feat')), may hold values from -6 to 6
- measured_signals: bfloat16 [256, 16384], P('tm', 'vox'), may hold values from -6 to 6
- predictor_group_label: int32 [4096], P('vox'), may hold values from 0 to 3
- shrinkage_weights: float32 [2, 4], replicated, may hold values from 0.1 to 10
- target_shrink_choice: int32 [256], P('vox'), may hold values from 0 to 1
Outputs:
- trailing: float32 [2, 4096, 4096], P(None, ('tm', 'feat'), 'vox')
- right_sides: float32 [4096, 16384], P(('tm', 'feat'), 'vox')
All inputs are finite; a program needn't handle non-finite values.
Results may differ from a plain program's by a relative error of at most 0.0003.
Values may be sent and summed in bfloat16 or wider, within the bound.
No kernel may reach another device: no remote copies, remote signals or barrier semaphores. Data moves between devices by JAX's collectives and lax.ppermute only.
A program may use at most 128 MiB of HBM per device.

v0:
```python
import jax
import jax.numpy as jnp
from jax import lax
from jax.experimental import pallas as pl
from jax.experimental.pallas import tpu as pltpu
from jax.sharding import PartitionSpec as P

GROUP = 64
F32 = jnp.float32
BF16 = jnp.bfloat16
HI = lax.Precision.HIGHEST
FIRST = (((0,), (0,)), ((), ()))
LANES = 128
B = 64
AXES = ("tm", "vox", "feat")


def lane_b(v, index):
    return jnp.take_along_axis(v, index, axis=1, mode="promise_in_bounds")


def sub_b(v, row):
    return jnp.broadcast_to(v[row : row + 1, :], v.shape)


def inverse_factors(tile):
    n = B // 8
    lanes = lax.broadcasted_iota(jnp.int32, (8, LANES), 1)
    subs = lax.broadcasted_iota(jnp.int32, (8, LANES), 0)
    base = jnp.where(lanes < B, 0, B)
    lane = lanes - base
    st = [tile[8 * i : 8 * i + 8, :] for i in range(n)]
    done = []
    for s in range(n):
        index = [base + (8 * s + j) for j in range(8)]
        pivot = (lane >= 8 * s) & (lane < 8 * s + 8)
        c = [lane_b(st[s], index[j]) for j in range(8)]
        row = jnp.where(pivot, jnp.where(lane - 8 * s == subs, 1.0, 0.0), st[s])
        out = row
        for j in range(8):
            d = sub_b(c[j], j)
            recip = 1.0 / d
            here = subs == j
            rb = sub_b(row, j)
            out = jnp.where(here, rb * lax.rsqrt(d), out)
            scaled = rb * recip
            row = jnp.where(here, scaled, row - c[j] * scaled)
            for l in range(j + 1, 8):
                scaled = sub_b(c[l], j) * recip
                c[l] = jnp.where(here, scaled, c[l] - c[j] * scaled)
        done.append(jnp.where(lane < 8 * s + 8, out, 0.0))
        if s + 1 < n:
            v = [sub_b(row, j) for j in range(8)]
            for t in range(s + 1, n):
                acc = jnp.where(pivot, 0.0, st[t])
                for j in range(8):
                    acc = acc - lane_b(st[t], index[j]) * v[j]
                st[t] = acc
    return jnp.concatenate(done, axis=0)


def split3(v):
    high = v.astype(BF16)
    rest = v - high.astype(F32)
    mid = rest.astype(BF16)
    return high, mid, (rest - mid.astype(F32)).astype(BF16)


def resident(v):
    return pltpu.with_memory_space_constraint(v, pltpu.VMEM)


def split(v):
    high = v.astype(BF16)
    return high, (v - high.astype(F32)).astype(BF16)


def factor_kernel(weights_ref, own_ref, mine_ref, last_ref, *refs):
    firsts, refs = refs[:-11], refs[-11:]
    w_out, k_out, xt_out = refs[:3]
    ws_ref, ks_ref, k_ref, xt_ref, x_ref, label_ref, xo_ref, sems = refs[3:]
    member = lax.axis_index(("tm", "feat"))
    vox = lax.axis_index("vox")
    width = mine_ref.shape[1]

    @pl.when(member == 0)
    def _():
        x_ref[...] = own_ref[:, :width]

    for s in range(len(firsts)):

        @pl.when(member == s + 1)
        def _():
            pltpu.sync_copy(firsts[s], x_ref)

    @pl.when(lax.rem(vox, 2) == 1)
    def _():
        pltpu.sync_copy(last_ref, label_ref)

    @pl.when(lax.rem(vox, 2) == 0)
    def _():
        pltpu.sync_copy(mine_ref, label_ref)

    groups = weights_ref.shape[1]
    time = x_ref.shape[0]
    blocks = width // B
    copies = []

    def send(source, target):
        copies.append(pltpu.make_async_copy(source, target, sems.at[len(copies)]))
        copies[-1].start()

    iota = lambda d, shape: lax.broadcasted_iota(jnp.int32, shape, d)
    eye = jnp.where(iota(0, (time, time)) == iota(1, (time, time)), 1.0, 0.0)
    xt_ref[...] = lax.dot_general(
        x_ref[...], eye.astype(BF16), FIRST, preferred_element_type=F32
    ).astype(BF16)
    low = iota(1, (B, LANES)) < B
    diagonal = iota(1, (B, LANES)) - jnp.where(low, 0, B) == iota(0, (B, LANES))

    def rows(n):
        return slice(n * B, (n + 1) * B)

    def chunk(n):
        return slice(n // 2 * LANES, (n // 2 + 1) * LANES)

    def pair(first, second, n):
        move = 1 - n % 2
        both = [first, second]
        both[move] = pltpu.roll(both[move], B, 1)
        return both

    def ridge(n):
        label = jnp.broadcast_to(label_ref[:, chunk(n)], (8, LANES))
        both = []
        for r in range(2):
            value = jnp.zeros((8, LANES), F32)
            for g in range(groups):
                value = jnp.where(label == g, weights_ref[r, g], value)
            both.append(value)
        both = pair(*both, n)
        return jnp.where(diagonal, jnp.where(low, both[0][:1], both[1][:1]), 0.0)

    def thrice(left, right):
        parts = [jnp.dot(left, p, preferred_element_type=F32) for p in split3(right)]
        return parts[0] + (parts[1] + parts[2])

    def thrice_left(left, right):
        m = left.shape[0]
        parts = jnp.dot(jnp.concatenate(split3(left), axis=0), right, preferred_element_type=F32)
        return parts[:m] + (parts[m : 2 * m] + parts[2 * m :])

    def schur(n, products):
        both = pair(*products, n)
        return jnp.where(low, both[0], both[1]) * (1.0 / time) + ridge(n)

    def coupling(n, products):
        both = pair(*products, n)
        return jnp.concatenate(
            [jnp.where(low, both[0], 0.0), jnp.where(low, 0.0, both[1])], axis=0
        ) * (1.0 / time)

    zeros = jnp.zeros((B, time), F32)
    gram = jnp.dot(xt_ref[rows(0), :], x_ref[:, chunk(0)], preferred_element_type=F32)
    tile = schur(0, [gram, gram])
    xt = xt_ref[: 2 * B, :]
    both = jnp.dot(xt, x_ref[:, chunk(1)], preferred_element_type=F32)
    q = [xt[:B].astype(F32)] * 2
    across = coupling(1, [both[:B]] * 2)
    ahead = schur(1, [both[B:]] * 2)
    for n in range(blocks):
        inverse = inverse_factors(tile)
        if n + 1 < blocks:
            p = jnp.dot(inverse, across, precision=HI, preferred_element_type=F32)
            pp = lax.dot_general(p, p, FIRST, precision=HI, preferred_element_type=F32)
            tile = ahead - jnp.where(low, pp[:B], pp[B:])
        for r in range(2):
            rhs = jnp.concatenate([q[0], zeros] if r == 0 else [zeros, q[1]], axis=0)
            w = jnp.dot(inverse, rhs, precision=HI, preferred_element_type=F32) * time**-0.5
            at = 2 * r * time
            ws_ref[rows(n), at : at + time], ws_ref[rows(n), at + time : at + 2 * time] = split(w)
            ww = lax.dot_general(w, w, FIRST, precision=HI, preferred_element_type=F32)
            k_ref[r] = (eye if n == 0 else k_ref[r]) - ww
        if n == 0:
            xo_ref[...] = lax.dot_general(
                own_ref[...], eye.astype(BF16), FIRST, preferred_element_type=F32
            ).astype(BF16)
        if n + 1 < blocks:
            last = n + 2 >= blocks
            xt = xt_ref[(n + 1) * B : (n + (2 if last else 3)) * B, :]
            qq = [thrice(xt, k_ref[r]) for r in range(2)]
            q = [v[:B] for v in qq]
            if not last:
                both = [thrice_left(v, x_ref[:, chunk(n + 2)]) for v in qq]
                across = coupling(n + 2, [v[:B] for v in both])
                ahead = schur(n + 2, [v[B:] for v in both])
    for r in range(2):
        at = 2 * r * time
        ks_ref[:, at : at + time], ks_ref[:, at + time : at + 2 * time] = split(k_ref[r])
    send(ks_ref, k_out)
    send(xo_ref, xt_out)

    @pl.when(member == 0)
    def _():
        pltpu.sync_copy(ws_ref, w_out)

    for c in copies:
        c.wait()


def factor(weights, x, labels, last, firsts):
    time, rows = x.shape
    width = labels.shape[1]
    stack = 2 * weights.shape[0] * time
    vmem = pl.BlockSpec(memory_space=pltpu.VMEM)
    hbm = pl.BlockSpec(memory_space=pl.ANY)
    return pl.pallas_call(
        factor_kernel,
        out_shape=(
            jax.ShapeDtypeStruct((width, stack), BF16),
            jax.ShapeDtypeStruct((time, stack), BF16),
            jax.ShapeDtypeStruct((rows, time), BF16),
        ),
        in_specs=[pl.BlockSpec(memory_space=pltpu.SMEM), vmem, hbm, hbm] + [hbm] * len(firsts),
        out_specs=(hbm, hbm, hbm),
        scratch_shapes=[
            pltpu.VMEM((width, stack), BF16),
            pltpu.VMEM((time, stack), BF16),
            pltpu.VMEM((2, time, time), F32),
            pltpu.VMEM((width, time), BF16),
            pltpu.VMEM((time, width), BF16),
            pltpu.VMEM((1, width), jnp.int32),
            pltpu.VMEM((rows, time), BF16),
            pltpu.SemaphoreType.DMA((2,)),
        ],
        name="factor",
    )(weights, x, labels, last, *firsts)


def apply_kernel(members, weights_ref, choice_ref, label_ref, x_hbm, xt_hbm, w_hbm, k_hbm, *refs):
    got_refs, y_hbms = refs[: members - 1], refs[members - 1 : -9]
    trail_ref, right_ref, xt_ref, xc_ref, ks_ref, ws_ref, y_ref, ym_ref, sems = refs[-9:]
    options, groups = weights_ref.shape
    rows = xt_hbm.shape[0]
    time, width = xc_ref.shape
    tile = right_ref.shape[1]
    n = len(y_hbms)
    part = time // n
    step = pl.program_id(0)
    member = lax.axis_index(("tm", "feat"))
    vox = lax.axis_index("vox")
    tm = lax.axis_index("tm")
    owner = vox * width // rows
    offset = vox * width - owner * rows

    early = [
        pltpu.make_async_copy(k_hbm, ks_ref, sems.at[0]),
        pltpu.make_async_copy(xt_hbm, xt_ref, sems.at[1]),
    ]
    late = [
        pltpu.make_async_copy(
            y_hbms[s],
            y_ref.at[pl.ds(pl.multiple_of(lax.rem(tm - s + n, n) * part, part), part), :],
            sems.at[2 + s],
        )
        for s in range(n)
    ]
    rest = pltpu.make_async_copy(w_hbm, ws_ref, sems.at[2 + n])

    @pl.when(step == 0)
    def _():
        for c in early + late:
            c.start()

        @pl.when(member == 0)
        def _():
            rest.start()

        @pl.when(owner == member)
        def _():
            pltpu.sync_copy(x_hbm.at[:, pl.ds(pl.multiple_of(offset, LANES), width)], xc_ref)

        for s in range(1, members):

            @pl.when(lax.rem(member - owner + members, members) == s)
            def _():
                pltpu.sync_copy(got_refs[s - 1], xc_ref)

        for c in early:
            c.wait()

    @pl.when(step == options)
    def _():
        for c in late:
            c.wait()

        @pl.when(member == 0)
        def _():
            rest.wait()

    def write(out_ref, z):
        high, low = split(z)

        def product(xt):
            return jnp.dot(xt, high, preferred_element_type=F32) + jnp.dot(
                xt, low, preferred_element_type=F32
            )

        @pl.when(member == 0)
        def _():
            out_ref[width:, :] = product(xt_ref[width:, :])

        @pl.when(member > 0)
        def _():
            out_ref[...] = product(xt_ref[...])

    @pl.when(step < options)
    def _():
        out_ref = trail_ref.at[0]

        @pl.when(vox == 0)
        def _():
            out_ref[...] = jnp.zeros_like(out_ref)

        @pl.when(vox > 0)
        def _():
            at = pl.ds(pl.multiple_of(step * 2 * time, LANES), 2 * time)
            xc = xc_ref[...]
            z = jnp.dot(ks_ref[:, at], jnp.concatenate([xc, xc], axis=0), preferred_element_type=F32)
            write(out_ref, z * (1.0 / time))

            @pl.when(member == 0)
            def _():
                out_ref[:width, :] = jnp.zeros((width, width), F32)

            @pl.when(owner == member)
            def _():
                to = pl.ds(pl.multiple_of(offset, LANES), width)
                ridge = jnp.zeros((1, width), F32)
                for g in range(groups):
                    ridge = jnp.where(label_ref[...] == g, weights_ref[step, g], ridge)
                row = lax.broadcasted_iota(jnp.int32, (width, width), 0)
                col = lax.broadcasted_iota(jnp.int32, (width, width), 1)
                out_ref[to, :] += jnp.where(row == col, ridge, 0.0)

    @pl.when(step >= options)
    def _():
        start = (step - options) * tile
        lane = lax.broadcasted_iota(jnp.int32, (1, LANES), 1)
        chosen = []
        for c in range(tile // LANES):
            value = jnp.zeros((1, LANES), F32)
            for i in range(LANES // GROUP):
                choice = choice_ref[start // GROUP + c * (LANES // GROUP) + i].astype(F32)
                value = jnp.where(lane >= i * GROUP, choice, value)
            chosen.append(value)
        chosen = jnp.concatenate(chosen, axis=1)
        y = y_ref[:, pl.ds(pl.multiple_of(start, LANES), tile)].astype(F32)
        for r in range(options):
            masked = jnp.where(chosen == float(r), y, 0.0).astype(BF16)
            for h in range(2):
                to = (2 * r + h) * time
                ym_ref[to : to + time, :] = masked
        ym = ym_ref[...]
        write(right_ref, jnp.dot(ks_ref[...], ym, preferred_element_type=F32) * time**-0.5)

        @pl.when(member == 0)
        def _():
            right_ref[:width, :] = jnp.dot(ws_ref[...], ym, preferred_element_type=F32)


def apply(weights, choice, labels, x, xt, w, k, gots, ys):
    rows, time = xt.shape
    width = labels.shape[1]
    voxels = ys[0].shape[1]
    options = weights.shape[0]
    tile = min(512, voxels)
    stack = 2 * options * time
    smem = pl.BlockSpec(memory_space=pltpu.SMEM)
    vmem = pl.BlockSpec(memory_space=pltpu.VMEM)
    hbm = pl.BlockSpec(memory_space=pl.ANY)
    return pl.pallas_call(
        lambda *refs: apply_kernel(len(gots) + 1, *refs),
        grid=(options + voxels // tile,),
        out_shape=(
            jax.ShapeDtypeStruct((options, rows, width), F32),
            jax.ShapeDtypeStruct((rows, voxels), F32),
        ),
        in_specs=[smem, smem, vmem] + [hbm] * (4 + len(gots) + len(ys)),
        out_specs=(
            pl.BlockSpec((1, rows, width), lambda s: (jnp.minimum(s, options - 1), 0, 0)),
            pl.BlockSpec((rows, tile), lambda s: (0, jnp.maximum(s - options, 0))),
        ),
        scratch_shapes=[
            pltpu.VMEM((rows, time), BF16),
            pltpu.VMEM((time, width), BF16),
            pltpu.VMEM((time, stack), BF16),
            pltpu.VMEM((width, stack), BF16),
            pltpu.VMEM((time, voxels), BF16),
            pltpu.VMEM((stack, tile), BF16),
            pltpu.SemaphoreType.DMA((3 + len(ys),)),
        ],
        name="apply",
    )(weights, choice, labels, x, xt, w, k, *gots, *ys)


def local(
    design_matrix, measured_signals, predictor_group_label, shrinkage_weights, target_shrink_choice
):
    nt, nv, nf = (lax.axis_size(a) for a in AXES)
    members = nt * nf
    vox = lax.axis_index("vox")
    rows = design_matrix.shape[1]
    width = predictor_group_label.shape[0]

    def device(g, v):
        return (g // nf * nv + v) * nf + g % nf

    def share(block, owner):
        gots = []
        for s in range(1, members):
            pairs = [(device(owner(v), v), device((owner(v) + s) % members, v)) for v in range(nv)]
            gots.append(lax.ppermute(block, AXES, pairs))
        small = len(gots) * block.size * block.dtype.itemsize <= 2**20
        return [resident(got) for got in gots] if small else gots

    firsts = share(design_matrix[:, :width], lambda v: 0)
    labels = predictor_group_label[None, :]
    stride = nv
    while stride > 1:
        half = stride // 2
        got = lax.ppermute(labels, "vox", [(a, a + half) for a in range(0, nv, stride)])
        if half > 1:
            labels = jnp.where(vox % stride == half, got, labels)
        stride = half
    ys = [measured_signals]
    for s in range(1, nt):
        pairs = [(a, (a + s) % nt) for a in range(nt)]
        ys.append(resident(lax.ppermute(measured_signals, "tm", pairs)))
    source = vox * width // rows
    own = lax.dynamic_slice_in_dim(design_matrix, vox * width - source * rows, width, 1)
    columns = share(own, lambda v: v * width // rows)

    w, k, xt = factor(
        shrinkage_weights, design_matrix, resident(labels), resident(got), firsts
    )
    return apply(
        shrinkage_weights,
        target_shrink_choice,
        predictor_group_label[None, :],
        design_matrix,
        xt,
        w,
        k,
        columns,
        ys,
    )


def solution(mesh):
    return jax.shard_map(
        local,
        mesh=mesh,
        in_specs=(P(None, ("tm", "feat")), P("tm", "vox"), P("vox"), P(), P("vox")),
        out_specs=(P(None, ("tm", "feat"), "vox"), P(("tm", "feat"), "vox")),
        check_vma=False,
    )
```

profile of v0, /device:TPU:0, one launch (start us, length us, event | category | flops | bytes accessed | tf_op | source)
XLA Modules:
  0.0 60.9 jit_solution(1988242539464579707)
XLA Ops:
  0.6 6.0 %collective-permute-start = (s32[1,512]{1,0:T(1,128)}, s32[1,512]{1,0:T(1,128)S(1)}, u32[]{:S(2)}, u32[]{:S(2)}) collective-permute-start(s32[1,512]{1,0:T(1,128)} %bitcast.1), channel_id=1, source_target_pairs={{0,8},{1,9},{16,24},{17,25}} | collective-permute-start | bytes 6152 | tf_op jit(solution)/shard_map/ppermute | solution.py:432
  6.6 1.1 %constant_dynamic-slice_fusion = (bf16[256,512]{1,0:T(8,128)(2,1)S(1)}, bf16[256,512]{1,0:T(8,128)(2,1)S(1)}) fusion(bf16[256,1024]{1,0:T(8,128)(2,1)} %refs_3_.1, s32[]{:T(128)S(6)} %select_n.39), kind=kLoop, calls=%fused_computation.2 | loop fusion | bytes 1048580 | tf_op jit(solution)/shard_map/dynamic_slice | solution.py:441
  7.8 2.6 %collective-permute-start.5 = (bf16[256,512]{1,0:T(8,128)(2,1)S(1)}, bf16[256,512]{1,0:T(8,128)(2,1)S(1)}, u32[]{:S(2)}, u32[]{:S(2)}) collective-permute-start(bf16[256,512]{1,0:T(8,128)(2,1)S(1)} %get-tuple-element.9), channel_id=1, source_target_pairs={{0,17},{2,19},{4,21},{6,23},{8,25},{10,27},{12,29},{14,31}} | collective-permute-start | bytes 786440 | tf_op jit(solution)/shard_map/ppermute | solution.py:423
  10.3 1.5 %collective-permute-start.4 = (bf16[256,512]{1,0:T(8,128)(2,1)S(1)}, bf16[256,512]{1,0:T(8,128)(2,1)S(1)}, u32[]{:S(2)}, u32[]{:S(2)}) collective-permute-start(bf16[256,512]{1,0:T(8,128)(2,1)S(1)} %get-tuple-element.9), channel_id=1, source_target_pairs={{0,16},{2,18},{4,20},{6,22},{8,24},{10,26},{12,28},{14,30}} | collective-permute-start | bytes 786440 | tf_op jit(solution)/shard_map/ppermute | solution.py:423
  11.9 0.1 collective-permute-start.9
  12.0 0.0 collective-permute-done
  12.0 0.7 %broadcast_select_fusion = s32[1,512]{1,0:T(1,128)S(1)} fusion(s32[1,512]{1,0:T(1,128)S(1)} %collective-permute-done, s32[1,512]{1,0:T(1,128)} %bitcast.2, pred[]{:T(512)S(6)} %eq.10), kind=kLoop, calls=%fused_computation | loop fusion | flops 512 | bytes 6145 | tf_op jit(solution)/shard_map/jit(_where)/select_n | solution.py:434
  12.7 1.3 %collective-permute-start.1 = (s32[1,512]{1,0:T(1,128)S(1)}, s32[1,512]{1,0:T(1,128)S(1)}, u32[]{:S(2)}, u32[]{:S(2)}) collective-permute-start(s32[1,512]{1,0:T(1,128)S(1)} %broadcast_select_fusion), channel_id=1, source_target_pairs={{0,4},{8,12},{1,5},{9,13},{16,20},{24,28},{17,21},{25,29}} | collective-permute-start | bytes 6152 | tf_op jit(solution)/shard_map/ppermute | solution.py:432
  14.0 1.3 %collective-permute-done.1 = s32[1,512]{1,0:T(1,128)S(1)} collective-permute-done((s32[1,512]{1,0:T(1,128)S(1)}, s32[1,512]{1,0:T(1,128)S(1)}, u32[]{:S(2)}, u32[]{:S(2)}) %collective-permute-start.1) | collective-permute-done | bytes 2080 | tf_op jit(solution)/shard_map/ppermute | solution.py:432
  15.2 1.3 %collective-permute-start.2 = (s32[1,512]{1,0:T(1,128)S(1)}, s32[1,512]{1,0:T(1,128)S(1)}, u32[]{:S(2)}, u32[]{:S(2)}) collective-permute-start(s32[1,512]{1,0:T(1,128)S(1)} %broadcast_select_fusion.1.mine_ref), channel_id=1, source_target_pairs={{0,2},{4,6},{8,10},{12,14},{1,3},{5,7},{9,11},{13,15},{16,18},{20,... | collective-permute-start | bytes 6152 | tf_op jit(solution)/shard_map/ppermute | solution.py:432
  16.5 1.3 %collective-permute-start.3 = (bf16[256,512]{1,0:T(8,128)(2,1)S(1)}, bf16[256,512]{1,0:T(8,128)(2,1)S(1)}, u32[]{:S(2)}, u32[]{:S(2)}) collective-permute-start(bf16[256,512]{1,0:T(8,128)(2,1)S(1)} %get-tuple-element.9), channel_id=1, source_target_pairs={{0,1},{2,3},{4,5},{6,7},{8,9},{10,11},{12,13},{14,15}} | collective-permute-start | bytes 786440 | tf_op jit(solution)/shard_map/ppermute | solution.py:423
  17.8 0.0 collective-permute-done.2.last_ref
  17.9 1.3 %collective-permute-start.8 = (bf16[256,512]{1,0:T(8,128)(2,1)S(1)}, bf16[256,512]{1,0:T(8,128)(2,1)S(1)}, u32[]{:S(2)}, u32[]{:S(2)}) collective-permute-start(bf16[256,512]{1,0:T(8,128)(2,1)S(1)} %get-tuple-element.8), channel_id=1, source_target_pairs={{0,17},{2,19},{5,4},{7,6},{24,9},{26,11},{29,28},{31,30}} | collective-permute-start | bytes 786440 | tf_op jit(solution)/shard_map/ppermute | solution.py:423
  19.2 0.0 collective-permute-done.5.refs_2_
  19.2 3.2 %collective-permute-start.7 = (bf16[256,512]{1,0:T(8,128)(2,1)S(1)}, bf16[256,512]{1,0:T(8,128)(2,1)S(1)}, u32[]{:S(2)}, u32[]{:S(2)}) collective-permute-start(bf16[256,512]{1,0:T(8,128)(2,1)S(1)} %get-tuple-element.8), channel_id=1, source_target_pairs={{0,16},{2,18},{5,21},{7,23},{24,8},{26,10},{29,13},{31,15}} | collective-permute-start | bytes 786440 | tf_op jit(solution)/shard_map/ppermute | solution.py:423
  22.4 0.0 collective-permute-done.4.refs_1_
  22.4 1.3 %collective-permute-start.6 = (bf16[256,512]{1,0:T(8,128)(2,1)S(1)}, bf16[256,512]{1,0:T(8,128)(2,1)S(1)}, u32[]{:S(2)}, u32[]{:S(2)}) collective-permute-start(bf16[256,512]{1,0:T(8,128)(2,1)S(1)} %get-tuple-element.8), channel_id=1, source_target_pairs={{0,1},{2,3},{5,20},{7,22},{24,25},{26,27},{29,12},{31,14}} | collective-permute-start | bytes 786440 | tf_op jit(solution)/shard_map/ppermute | solution.py:423
  23.7 0.0 collective-permute-done.3.refs_0_
  23.8 24.2 %factor.1 = (bf16[512,1024]{1,0:T(8,128)(2,1)}, bf16[256,1024]{1,0:T(8,128)(2,1)}, bf16[1024,256]{1,0:T(8,128)(2,1)}) custom-call(f32[2,4]{1,0:T(2,128)} %refs_0_.1, bf16[256,1024]{1,0:T(8,128)(2,1)} %refs_3_.1, s32[1,512]{1,0:T(1,128)S(1)} %broadcast_select_fusion.1.mine_ref, s32[1,512]{1,0:T(1,128)S(1)} %collective-permute-done.2.last_ref, ...), custom_call_target="tpu_custom_call" | custom-call | tf_op jit(solution)/shard_map/factor/pallas_call | solution.py:217
  48.0 0.0 collective-permute-done.8.refs_9_
  48.0 0.0 collective-permute-done.7.refs_8_
  48.0 0.0 collective-permute-done.6.refs_7_
  48.0 0.0 collective-permute-done.9.refs_11_
  48.0 12.7 %apply.1 = (f32[2,1024,512]{2,1,0:T(8,128)}, f32[1024,2048]{1,0:T(8,128)}) custom-call(f32[2,4]{1,0:T(2,128)} %refs_0_.1, s32[32]{0:T(128)} %refs_1_.1, s32[1,512]{1,0:T(1,128)} %bitcast.3, bf16[256,1024]{1,0:T(8,128)(2,1)} %refs_3_.1, bf16[1024,256]{1,0:T(8,128)(2,1)} %get-tuple-element.5.refs_4_, bf16[512,1024]{1,0:T(8,128)(2,1)} %get-tuple-element.6.refs_5_, ...), custom_call_target="tpu_custom_call" | custom-call | tf_op jit(solution)/shard_map/apply/pallas_call | solution.py:382
  (1 shorter events, 0.0 us)
Async XLA Ops:
  0.6 11.3 %collective-permute-start = (s32[1,512]{1,0:T(1,128)}, s32[1,512]{1,0:T(1,128)S(1)}, u32[]{:S(2)}, u32[]{:S(2)}) collective-permute-start(s32[1,512]{1,0:T(1,128)} %bitcast.1), channel_id=1, source_target_pairs={{0,8},{1,9},{16,24},{17,25}} | collective-permute-start | bytes 6152 | tf_op jit(solution)/shard_map/ppermute | solution.py:432
  7.8 11.4 %collective-permute-start.5 = (bf16[256,512]{1,0:T(8,128)(2,1)S(1)}, bf16[256,512]{1,0:T(8,128)(2,1)S(1)}, u32[]{:S(2)}, u32[]{:S(2)}) collective-permute-start(bf16[256,512]{1,0:T(8,128)(2,1)S(1)} %get-tuple-element.9), channel_id=1, source_target_pairs={{0,17},{2,19},{4,21},{6,23},{8,25},{10,27},{12,29},{14,31}} | collective-permute-start | bytes 786440 | tf_op jit(solution)/shard_map/ppermute | solution.py:423
  10.3 12.1 %collective-permute-start.4 = (bf16[256,512]{1,0:T(8,128)(2,1)S(1)}, bf16[256,512]{1,0:T(8,128)(2,1)S(1)}, u32[]{:S(2)}, u32[]{:S(2)}) collective-permute-start(bf16[256,512]{1,0:T(8,128)(2,1)S(1)} %get-tuple-element.9), channel_id=1, source_target_pairs={{0,16},{2,18},{4,20},{6,22},{8,24},{10,26},{12,28},{14,30}} | collective-permute-start | bytes 786440 | tf_op jit(solution)/shard_map/ppermute | solution.py:423
  11.9 36.2 %collective-permute-start.9 = (bf16[128,2048]{1,0:T(8,128)(2,1)}, bf16[128,2048]{1,0:T(8,128)(2,1)S(1)}, u32[]{:S(2)}, u32[]{:S(2)}) collective-permute-start(bf16[128,2048]{1,0:T(8,128)(2,1)} %refs_10_.1), channel_id=1, source_target_pairs={{0,16},{16,0},{1,17},{17,1},{2,18},{18,2},{3,19},{19,3},{4,20},{20... | collective-permute-start | bytes 1572872 | tf_op jit(solution)/shard_map/ppermute | solution.py:439
  12.7 2.6 %collective-permute-start.1 = (s32[1,512]{1,0:T(1,128)S(1)}, s32[1,512]{1,0:T(1,128)S(1)}, u32[]{:S(2)}, u32[]{:S(2)}) collective-permute-start(s32[1,512]{1,0:T(1,128)S(1)} %broadcast_select_fusion), channel_id=1, source_target_pairs={{0,4},{8,12},{1,5},{9,13},{16,20},{24,28},{17,21},{25,29}} | collective-permute-start | bytes 6152 | tf_op jit(solution)/shard_map/ppermute | solution.py:432
  15.2 2.6 %collective-permute-start.2 = (s32[1,512]{1,0:T(1,128)S(1)}, s32[1,512]{1,0:T(1,128)S(1)}, u32[]{:S(2)}, u32[]{:S(2)}) collective-permute-start(s32[1,512]{1,0:T(1,128)S(1)} %broadcast_select_fusion.1.mine_ref), channel_id=1, source_target_pairs={{0,2},{4,6},{8,10},{12,14},{1,3},{5,7},{9,11},{13,15},{16,18},{20,... | collective-permute-start | bytes 6152 | tf_op jit(solution)/shard_map/ppermute | solution.py:432
  16.5 7.2 %collective-permute-start.3 = (bf16[256,512]{1,0:T(8,128)(2,1)S(1)}, bf16[256,512]{1,0:T(8,128)(2,1)S(1)}, u32[]{:S(2)}, u32[]{:S(2)}) collective-permute-start(bf16[256,512]{1,0:T(8,128)(2,1)S(1)} %get-tuple-element.9), channel_id=1, source_target_pairs={{0,1},{2,3},{4,5},{6,7},{8,9},{10,11},{12,13},{14,15}} | collective-permute-start | bytes 786440 | tf_op jit(solution)/shard_map/ppermute | solution.py:423
  17.9 30.1 %collective-permute-start.8 = (bf16[256,512]{1,0:T(8,128)(2,1)S(1)}, bf16[256,512]{1,0:T(8,128)(2,1)S(1)}, u32[]{:S(2)}, u32[]{:S(2)}) collective-permute-start(bf16[256,512]{1,0:T(8,128)(2,1)S(1)} %get-tuple-element.8), channel_id=1, source_target_pairs={{0,17},{2,19},{5,4},{7,6},{24,9},{26,11},{29,28},{31,30}} | collective-permute-start | bytes 786440 | tf_op jit(solution)/shard_map/ppermute | solution.py:423
  19.2 28.8 %collective-permute-start.7 = (bf16[256,512]{1,0:T(8,128)(2,1)S(1)}, bf16[256,512]{1,0:T(8,128)(2,1)S(1)}, u32[]{:S(2)}, u32[]{:S(2)}) collective-permute-start(bf16[256,512]{1,0:T(8,128)(2,1)S(1)} %get-tuple-element.8), channel_id=1, source_target_pairs={{0,16},{2,18},{5,21},{7,23},{24,8},{26,10},{29,13},{31,15}} | collective-permute-start | bytes 786440 | tf_op jit(solution)/shard_map/ppermute | solution.py:423
  22.4 25.6 %collective-permute-start.6 = (bf16[256,512]{1,0:T(8,128)(2,1)S(1)}, bf16[256,512]{1,0:T(8,128)(2,1)S(1)}, u32[]{:S(2)}, u32[]{:S(2)}) collective-permute-start(bf16[256,512]{1,0:T(8,128)(2,1)S(1)} %get-tuple-element.8), channel_id=1, source_target_pairs={{0,1},{2,3},{5,20},{7,22},{24,25},{26,27},{29,12},{31,14}} | collective-permute-start | bytes 786440 | tf_op jit(solution)/shard_map/ppermute | solution.py:423
where the time goes:
time: 61.3 us; the launch traced here: 60.9 us
  Pallas kernels  37 us (60%)
  starting transfers between devices  19.8 us (32%)
  waiting for transfers between devices  1.3 us (2%)
  local copies, waits for them, and re-layouts  1.13 us (2%)
  between operations  1 us (2%)
  other arithmetic  0.7 us (1%)
    pallas_call x1, Pallas kernels, factor(): pl.pallas_call(factor_kernel, out_shape=(jax.ShapeDtypeStruct((width, sta...  24.2 us
    pallas_call x1, Pallas kernels, apply(): pl.pallas_call(lambda *refs: apply_kernel(len(gots) + 1, *refs), grid=(op...  12.7 us
    ppermute x6, starting transfers between devices, share(): gots.append(lax.ppermute(block, AXES, pairs))  11.2 us
    ppermute x3, starting transfers between devices, local(): lax.ppermute(labels, 'vox', [(a, a + half) for a in range(0, nv, stride)])  8.53 us
    ppermute x3, waiting for transfers between devices, local(): lax.ppermute(labels, 'vox', [(a, a + half) for a in range(0, nv, stride)])  1.28 us
  transfers between devices with their start and end apart: 10, of which 1 were waited for; matrix products, arithmetic and copies ran while one was open for 3% of the time, Pallas kernels for 40%

commit v1 on v0

--- a/solution.py
+++ b/solution.py
@@ -8,7 +8,6 @@
 GROUP = 64
 F32 = jnp.float32
 BF16 = jnp.bfloat16
-HI = lax.Precision.HIGHEST
 FIRST = (((0,), (0,)), ((), ()))
 LANES = 128
 B = 64
@@ -75,6 +74,14 @@
     return high, (v - high.astype(F32)).astype(BF16)
 
 
+PRODUCTS = ((0, 0), (0, 1), (1, 0), (0, 2), (2, 0), (1, 1))
+
+
+def stack(v, side, axis):
+    parts = split3(v)
+    return jnp.concatenate([parts[p[side]] for p in PRODUCTS], axis=axis)
+
+
 def factor_kernel(weights_ref, own_ref, mine_ref, last_ref, *refs):
     firsts, refs = refs[:-11], refs[-11:]
     w_out, k_out, xt_out = refs[:3]
@@ -93,11 +100,13 @@
         def _():
             pltpu.sync_copy(firsts[s], x_ref)
 
-    @pl.when(lax.rem(vox, 2) == 1)
+    received = 2 * vox >= lax.axis_size("vox")
+
+    @pl.when(received)
     def _():
         pltpu.sync_copy(last_ref, label_ref)
 
-    @pl.when(lax.rem(vox, 2) == 0)
+    @pl.when(jnp.logical_not(received))
     def _():
         pltpu.sync_copy(mine_ref, label_ref)
 
@@ -169,17 +178,17 @@
     across = coupling(1, [both[:B]] * 2)
     ahead = schur(1, [both[B:]] * 2)
     for n in range(blocks):
-        inverse = inverse_factors(tile)
+        inverse = stack(inverse_factors(tile), 0, 1)
         if n + 1 < blocks:
-            p = jnp.dot(inverse, across, precision=HI, preferred_element_type=F32)
-            pp = lax.dot_general(p, p, FIRST, precision=HI, preferred_element_type=F32)
+            p = jnp.dot(inverse, stack(across, 1, 0), preferred_element_type=F32)
+            pp = lax.dot_general(stack(p, 0, 0), stack(p, 1, 0), FIRST, preferred_element_type=F32)
             tile = ahead - jnp.where(low, pp[:B], pp[B:])
         for r in range(2):
             rhs = jnp.concatenate([q[0], zeros] if r == 0 else [zeros, q[1]], axis=0)
-            w = jnp.dot(inverse, rhs, precision=HI, preferred_element_type=F32) * time**-0.5
+            w = jnp.dot(inverse, stack(rhs, 1, 0), preferred_element_type=F32) * time**-0.5
             at = 2 * r * time
             ws_ref[rows(n), at : at + time], ws_ref[rows(n), at + time : at + 2 * time] = split(w)
-            ww = lax.dot_general(w, w, FIRST, precision=HI, preferred_element_type=F32)
+            ww = lax.dot_general(stack(w, 0, 0), stack(w, 1, 0), FIRST, preferred_element_type=F32)
             k_ref[r] = (eye if n == 0 else k_ref[r]) - ww
         if n == 0:
             xo_ref[...] = lax.dot_general(
@@ -238,15 +247,14 @@
 
 
 def apply_kernel(members, weights_ref, choice_ref, label_ref, x_hbm, xt_hbm, w_hbm, k_hbm, *refs):
-    got_refs, y_hbms = refs[: members - 1], refs[members - 1 : -9]
-    trail_ref, right_ref, xt_ref, xc_ref, ks_ref, ws_ref, y_ref, ym_ref, sems = refs[-9:]
+    got_refs, y_hbms = refs[: members - 1], refs[members - 1 : -11]
+    trail_hbm, right_hbm = refs[-11:-9]
+    xt_ref, xc_ref, ks_ref, ws_ref, y_ref, ym_ref, out_ref, sems, sent = refs[-9:]
     options, groups = weights_ref.shape
-    rows = xt_hbm.shape[0]
+    tiles, rows, tile = out_ref.shape
     time, width = xc_ref.shape
-    tile = right_ref.shape[1]
     n = len(y_hbms)
     part = time // n
-    step = pl.program_id(0)
     member = lax.axis_index(("tm", "feat"))
     vox = lax.axis_index("vox")
     tm = lax.axis_index("tm")
@@ -266,39 +274,27 @@
         for s in range(n)
     ]
     rest = pltpu.make_async_copy(w_hbm, ws_ref, sems.at[2 + n])
-
-    @pl.when(step == 0)
-    def _():
-        for c in early + late:
-            c.start()
-
-        @pl.when(member == 0)
-        def _():
-            rest.start()
-
-        @pl.when(owner == member)
-        def _():
-            pltpu.sync_copy(x_hbm.at[:, pl.ds(pl.multiple_of(offset, LANES), width)], xc_ref)
-
-        for s in range(1, members):
-
-            @pl.when(lax.rem(member - owner + members, members) == s)
-            def _():
-                pltpu.sync_copy(got_refs[s - 1], xc_ref)
-
-        for c in early:
-            c.wait()
-
-    @pl.when(step == options)
-    def _():
-        for c in late:
-            c.wait()
-
-        @pl.when(member == 0)
-        def _():
-            rest.wait()
-
-    def write(out_ref, z):
+    for c in early + late:
+        c.start()
+
+    @pl.when(member == 0)
+    def _():
+        rest.start()
+
+    @pl.when(owner == member)
+    def _():
+        pltpu.sync_copy(x_hbm.at[:, pl.ds(pl.multiple_of(offset, LANES), width)], xc_ref)
+
+    for s in range(1, members):
+
+        @pl.when(lax.rem(member - owner + members, members) == s)
+        def _():
+            pltpu.sync_copy(got_refs[s - 1], xc_ref)
+
+    for c in early:
+        c.wait()
+
+    def write(target, z):
         high, low = split(z)
 
         def product(xt):
@@ -308,44 +304,63 @@
 
         @pl.when(member == 0)
         def _():
-            out_ref[width:, :] = product(xt_ref[width:, :])
+            target[width:, :] = product(xt_ref[width:, :])
 
         @pl.when(member > 0)
         def _():
-            out_ref[...] = product(xt_ref[...])
-
-    @pl.when(step < options)
-    def _():
-        out_ref = trail_ref.at[0]
+            target[...] = product(xt_ref[...])
+
+    def trailing(r):
+        return pltpu.make_async_copy(out_ref.at[r, :, :width], trail_hbm.at[r], sent.at[r])
+
+    def sides(j):
+        at = pl.ds(pl.multiple_of(j * tile, LANES), tile)
+        return pltpu.make_async_copy(
+            out_ref.at[options + j], right_hbm.at[:, at], sent.at[options + j]
+        )
+
+    def system(r, _):
+        target = out_ref.at[r, :, :width]
 
         @pl.when(vox == 0)
         def _():
-            out_ref[...] = jnp.zeros_like(out_ref)
+            target[...] = jnp.zeros((rows, width), F32)
 
         @pl.when(vox > 0)
         def _():
-            at = pl.ds(pl.multiple_of(step * 2 * time, LANES), 2 * time)
+            at = pl.ds(pl.multiple_of(r * 2 * time, LANES), 2 * time)
             xc = xc_ref[...]
             z = jnp.dot(ks_ref[:, at], jnp.concatenate([xc, xc], axis=0), preferred_element_type=F32)
-            write(out_ref, z * (1.0 / time))
+            write(target, z * (1.0 / time))
 
             @pl.when(member == 0)
             def _():
-                out_ref[:width, :] = jnp.zeros((width, width), F32)
+                target[:width, :] = jnp.zeros((width, width), F32)
 
             @pl.when(owner == member)
             def _():
                 to = pl.ds(pl.multiple_of(offset, LANES), width)
                 ridge = jnp.zeros((1, width), F32)
                 for g in range(groups):
-                    ridge = jnp.where(label_ref[...] == g, weights_ref[step, g], ridge)
+                    ridge = jnp.where(label_ref[...] == g, weights_ref[r, g], ridge)
                 row = lax.broadcasted_iota(jnp.int32, (width, width), 0)
                 col = lax.broadcasted_iota(jnp.int32, (width, width), 1)
-                out_ref[to, :] += jnp.where(row == col, ridge, 0.0)
-
-    @pl.when(step >= options)
-    def _():
-        start = (step - options) * tile
+                target[to, :] += jnp.where(row == col, ridge, 0.0)
+
+        trailing(r).start()
+        return 0
+
+    lax.fori_loop(0, options, system, 0)
+    for c in late:
+        c.wait()
+
+    @pl.when(member == 0)
+    def _():
+        rest.wait()
+
+    def signals(j, _):
+        target = out_ref.at[options + j]
+        start = j * tile
         lane = lax.broadcasted_iota(jnp.int32, (1, LANES), 1)
         chosen = []
         for c in range(tile // LANES):
@@ -362,11 +377,20 @@
                 to = (2 * r + h) * time
                 ym_ref[to : to + time, :] = masked
         ym = ym_ref[...]
-        write(right_ref, jnp.dot(ks_ref[...], ym, preferred_element_type=F32) * time**-0.5)
+        write(target, jnp.dot(ks_ref[...], ym, preferred_element_type=F32) * time**-0.5)
 
         @pl.when(member == 0)
         def _():
-            right_ref[:width, :] = jnp.dot(ws_ref[...], ym, preferred_element_type=F32)
+            target[:width, :] = jnp.dot(ws_ref[...], ym, preferred_element_type=F32)
+
+        sides(j).start()
+        return 0
+
+    lax.fori_loop(0, tiles - options, signals, 0)
+    for r in range(options):
+        trailing(r).wait()
+    for j in range(tiles - options):
+        sides(j).wait()
 
 
 def apply(weights, choice, labels, x, xt, w, k, gots, ys):
@@ -375,22 +399,19 @@
     voxels = ys[0].shape[1]
     options = weights.shape[0]
     tile = min(512, voxels)
+    tiles = options + voxels // tile
     stack = 2 * options * time
     smem = pl.BlockSpec(memory_space=pltpu.SMEM)
     vmem = pl.BlockSpec(memory_space=pltpu.VMEM)
     hbm = pl.BlockSpec(memory_space=pl.ANY)
     return pl.pallas_call(
         lambda *refs: apply_kernel(len(gots) + 1, *refs),
-        grid=(options + voxels // tile,),
         out_shape=(
             jax.ShapeDtypeStruct((options, rows, width), F32),
             jax.ShapeDtypeStruct((rows, voxels), F32),
         ),
         in_specs=[smem, smem, vmem] + [hbm] * (4 + len(gots) + len(ys)),
-        out_specs=(
-            pl.BlockSpec((1, rows, width), lambda s: (jnp.minimum(s, options - 1), 0, 0)),
-            pl.BlockSpec((rows, tile), lambda s: (0, jnp.maximum(s - options, 0))),
-        ),
+        out_specs=(hbm, hbm),
         scratch_shapes=[
             pltpu.VMEM((rows, time), BF16),
             pltpu.VMEM((time, width), BF16),
@@ -398,7 +419,9 @@
             pltpu.VMEM((width, stack), BF16),
             pltpu.VMEM((time, voxels), BF16),
             pltpu.VMEM((stack, tile), BF16),
+            pltpu.VMEM((tiles, rows, max(tile, width)), F32),
             pltpu.SemaphoreType.DMA((3 + len(ys),)),
+            pltpu.SemaphoreType.DMA((tiles,)),
         ],
         name="apply",
     )(weights, choice, labels, x, xt, w, k, *gots, *ys)
@@ -426,13 +449,12 @@
 
     firsts = share(design_matrix[:, :width], lambda v: 0)
     labels = predictor_group_label[None, :]
-    stride = nv
-    while stride > 1:
-        half = stride // 2
-        got = lax.ppermute(labels, "vox", [(a, a + half) for a in range(0, nv, stride)])
-        if half > 1:
-            labels = jnp.where(vox % stride == half, got, labels)
-        stride = half
+    known = 1
+    while known < nv:
+        got = lax.ppermute(labels, "vox", [(a, a + known) for a in range(known)])
+        known *= 2
+        if known < nv:
+            labels = jnp.where((vox >= known // 2) & (vox < known), got, labels)
     ys = [measured_signals]
     for s in range(1, nt):
         pairs = [(a, (a + s) % nt) for a in range(nt)]

time: 61.3 us -> 56.5 us (0.922)
  Pallas kernels: 37 us -> 33.2 us
  starting transfers between devices: 19.8 us -> 18.8 us
    pallas_call x1, Pallas kernels: 12.7 us -> 10.6 us  [apply(): pl.pallas_call(lambda *refs: apply_kernel(len(gots) + 1, *refs), out_shap...]
    pallas_call x1, Pallas kernels: 24.2 us -> 22.6 us  [factor(): pl.pallas_call(factor_kernel, out_shape=(jax.ShapeDtypeStruct((width, sta...]
    ppermute x3, starting transfers between devices: 8.53 us -> 7.46 us  [local(): got = lax.ppermute(labels, 'vox', [(a, a + known) for a in range(known)])]
where the time goes in v1:
time: 56.5 us; the launch traced here: 56.1 us
  Pallas kernels  33.2 us (59%)
  starting transfers between devices  18.8 us (33%)
  waiting for transfers between devices  1.31 us (2%)
  local copies, waits for them, and re-layouts  1.13 us (2%)
  between operations  0.99 us (2%)
  other arithmetic  0.7 us (1%)
    pallas_call x1, Pallas kernels, factor(): pl.pallas_call(factor_kernel, out_shape=(jax.ShapeDtypeStruct((width, sta...  22.6 us
    ppermute x6, starting transfers between devices, share(): gots.append(lax.ppermute(block, AXES, pairs))  11.2 us
    pallas_call x1, Pallas kernels, apply(): pl.pallas_call(lambda *refs: apply_kernel(len(gots) + 1, *refs), out_shap...  10.6 us
    ppermute x3, starting transfers between devices, local(): got = lax.ppermute(labels, 'vox', [(a, a + known) for a in range(known)])  7.46 us
    ppermute x3, waiting for transfers between devices, local(): got = lax.ppermute(labels, 'vox', [(a, a + known) for a in range(known)])  1.29 us
    dynamic_slice x1, local copies, waits for them, and re-layouts, local(): lax.dynamic_slice_in_dim(design_matrix, vox * width - source * rows, widt...  1.13 us
  transfers between devices with their start and end apart: 10, of which 1 were waited for; matrix products, arithmetic and copies ran while one was open for 3% of the time, Pallas kernels for 40%

profile of v1, /device:TPU:0, one launch (start us, length us, event | category | flops | bytes accessed | tf_op | source)
XLA Modules:
  0.0 56.1 jit_solution(4823797632726516426)
XLA Ops:
  0.6 4.9 %collective-permute-start = (s32[1,512]{1,0:T(1,128)}, s32[1,512]{1,0:T(1,128)S(1)}, u32[]{:S(2)}, u32[]{:S(2)}) collective-permute-start(s32[1,512]{1,0:T(1,128)} %bitcast.1), channel_id=1, source_target_pairs={{0,2},{1,3},{16,18},{17,19}} | collective-permute-start | bytes 6152 | tf_op jit(solution)/shard_map/ppermute | solution.py:454
  5.6 1.1 %constant_dynamic-slice_fusion = (bf16[256,512]{1,0:T(8,128)(2,1)S(1)}, bf16[256,512]{1,0:T(8,128)(2,1)S(1)}) fusion(bf16[256,1024]{1,0:T(8,128)(2,1)} %refs_3_.1, s32[]{:T(128)S(6)} %select_n.27), kind=kLoop, calls=%fused_computation.2 | loop fusion | bytes 1048580 | tf_op jit(solution)/shard_map/dynamic_slice | solution.py:463
  6.7 2.6 %collective-permute-start.5 = (bf16[256,512]{1,0:T(8,128)(2,1)S(1)}, bf16[256,512]{1,0:T(8,128)(2,1)S(1)}, u32[]{:S(2)}, u32[]{:S(2)}) collective-permute-start(bf16[256,512]{1,0:T(8,128)(2,1)S(1)} %get-tuple-element.9), channel_id=1, source_target_pairs={{0,17},{2,19},{4,21},{6,23},{8,25},{10,27},{12,29},{14,31}} | collective-permute-start | bytes 786440 | tf_op jit(solution)/shard_map/ppermute | solution.py:446
  9.3 1.5 %collective-permute-start.4 = (bf16[256,512]{1,0:T(8,128)(2,1)S(1)}, bf16[256,512]{1,0:T(8,128)(2,1)S(1)}, u32[]{:S(2)}, u32[]{:S(2)}) collective-permute-start(bf16[256,512]{1,0:T(8,128)(2,1)S(1)} %get-tuple-element.9), channel_id=1, source_target_pairs={{0,16},{2,18},{4,20},{6,22},{8,24},{10,26},{12,28},{14,30}} | collective-permute-start | bytes 786440 | tf_op jit(solution)/shard_map/ppermute | solution.py:446
  10.8 0.1 collective-permute-start.9
  10.9 0.0 collective-permute-done
  10.9 0.7 %broadcast_select_fusion = s32[1,512]{1,0:T(1,128)S(1)} fusion(s32[1,512]{1,0:T(1,128)S(1)} %collective-permute-done, s32[1,512]{1,0:T(1,128)} %bitcast.2, pred[]{:T(512)S(6)} %and.13), kind=kLoop, calls=%fused_computation | loop fusion | flops 512 | bytes 6145 | tf_op jit(solution)/shard_map/jit(_where)/select_n | solution.py:457
  11.6 1.3 %collective-permute-start.1 = (s32[1,512]{1,0:T(1,128)S(1)}, s32[1,512]{1,0:T(1,128)S(1)}, u32[]{:S(2)}, u32[]{:S(2)}) collective-permute-start(s32[1,512]{1,0:T(1,128)S(1)} %broadcast_select_fusion), channel_id=1, source_target_pairs={{0,4},{2,6},{1,5},{3,7},{16,20},{18,22},{17,21},{19,23}} | collective-permute-start | bytes 6152 | tf_op jit(solution)/shard_map/ppermute | solution.py:454
  12.9 1.3 %collective-permute-done.1 = s32[1,512]{1,0:T(1,128)S(1)} collective-permute-done((s32[1,512]{1,0:T(1,128)S(1)}, s32[1,512]{1,0:T(1,128)S(1)}, u32[]{:S(2)}, u32[]{:S(2)}) %collective-permute-start.1) | collective-permute-done | bytes 2080 | tf_op jit(solution)/shard_map/ppermute | solution.py:454
  14.2 1.3 %collective-permute-start.2 = (s32[1,512]{1,0:T(1,128)S(1)}, s32[1,512]{1,0:T(1,128)S(1)}, u32[]{:S(2)}, u32[]{:S(2)}) collective-permute-start(s32[1,512]{1,0:T(1,128)S(1)} %broadcast_select_fusion.1.mine_ref), channel_id=1, source_target_pairs={{0,8},{2,10},{4,12},{6,14},{1,9},{3,11},{5,13},{7,15},{16,24},{18,... | collective-permute-start | bytes 6152 | tf_op jit(solution)/shard_map/ppermute | solution.py:454
  15.5 1.3 %collective-permute-start.3 = (bf16[256,512]{1,0:T(8,128)(2,1)S(1)}, bf16[256,512]{1,0:T(8,128)(2,1)S(1)}, u32[]{:S(2)}, u32[]{:S(2)}) collective-permute-start(bf16[256,512]{1,0:T(8,128)(2,1)S(1)} %get-tuple-element.9), channel_id=1, source_target_pairs={{0,1},{2,3},{4,5},{6,7},{8,9},{10,11},{12,13},{14,15}} | collective-permute-start | bytes 786440 | tf_op jit(solution)/shard_map/ppermute | solution.py:446
  16.8 0.0 collective-permute-done.2.last_ref
  16.8 1.3 %collective-permute-start.8 = (bf16[256,512]{1,0:T(8,128)(2,1)S(1)}, bf16[256,512]{1,0:T(8,128)(2,1)S(1)}, u32[]{:S(2)}, u32[]{:S(2)}) collective-permute-start(bf16[256,512]{1,0:T(8,128)(2,1)S(1)} %get-tuple-element.8), channel_id=1, source_target_pairs={{0,17},{2,19},{5,4},{7,6},{24,9},{26,11},{29,28},{31,30}} | collective-permute-start | bytes 786440 | tf_op jit(solution)/shard_map/ppermute | solution.py:446
  18.1 0.0 collective-permute-done.5.refs_2_
  18.1 3.2 %collective-permute-start.7 = (bf16[256,512]{1,0:T(8,128)(2,1)S(1)}, bf16[256,512]{1,0:T(8,128)(2,1)S(1)}, u32[]{:S(2)}, u32[]{:S(2)}) collective-permute-start(bf16[256,512]{1,0:T(8,128)(2,1)S(1)} %get-tuple-element.8), channel_id=1, source_target_pairs={{0,16},{2,18},{5,21},{7,23},{24,8},{26,10},{29,13},{31,15}} | collective-permute-start | bytes 786440 | tf_op jit(solution)/shard_map/ppermute | solution.py:446
  21.4 0.0 collective-permute-done.4.refs_1_
  21.4 1.3 %collective-permute-start.6 = (bf16[256,512]{1,0:T(8,128)(2,1)S(1)}, bf16[256,512]{1,0:T(8,128)(2,1)S(1)}, u32[]{:S(2)}, u32[]{:S(2)}) collective-permute-start(bf16[256,512]{1,0:T(8,128)(2,1)S(1)} %get-tuple-element.8), channel_id=1, source_target_pairs={{0,1},{2,3},{5,20},{7,22},{24,25},{26,27},{29,12},{31,14}} | collective-permute-start | bytes 786440 | tf_op jit(solution)/shard_map/ppermute | solution.py:446
  22.7 0.0 collective-permute-done.3.refs_0_
  22.7 22.6 %factor.1 = (bf16[512,1024]{1,0:T(8,128)(2,1)}, bf16[256,1024]{1,0:T(8,128)(2,1)}, bf16[1024,256]{1,0:T(8,128)(2,1)}) custom-call(f32[2,4]{1,0:T(2,128)} %refs_0_.1, bf16[256,1024]{1,0:T(8,128)(2,1)} %refs_3_.1, s32[1,512]{1,0:T(1,128)S(1)} %broadcast_select_fusion.1.mine_ref, s32[1,512]{1,0:T(1,128)S(1)} %collective-permute-done.2.last_ref, ...), custom_call_target="tpu_custom_call" | custom-call | tf_op jit(solution)/shard_map/factor/pallas_call | solution.py:226
  45.3 0.0 collective-permute-done.8.refs_9_
  45.3 0.0 collective-permute-done.7.refs_8_
  45.4 0.0 collective-permute-done.6.refs_7_
  45.4 0.0 collective-permute-done.9.refs_11_
  45.4 10.6 %apply.1 = (f32[2,1024,512]{2,1,0:T(8,128)}, f32[1024,2048]{1,0:T(8,128)}) custom-call(f32[2,4]{1,0:T(2,128)} %refs_0_.1, s32[32]{0:T(128)} %refs_1_.1, s32[1,512]{1,0:T(1,128)} %bitcast.3, bf16[256,1024]{1,0:T(8,128)(2,1)} %refs_3_.1, bf16[1024,256]{1,0:T(8,128)(2,1)} %get-tuple-element.5.refs_4_, bf16[512,1024]{1,0:T(8,128)(2,1)} %get-tuple-element.6.refs_5_, ...), custom_call_target="tpu_custom_call" | custom-call | tf_op jit(solution)/shard_map/apply/pallas_call | solution.py:407
  (1 shorter events, 0.0 us)
Async XLA Ops:
  0.6 10.3 %collective-permute-start = (s32[1,512]{1,0:T(1,128)}, s32[1,512]{1,0:T(1,128)S(1)}, u32[]{:S(2)}, u32[]{:S(2)}) collective-permute-start(s32[1,512]{1,0:T(1,128)} %bitcast.1), channel_id=1, source_target_pairs={{0,2},{1,3},{16,18},{17,19}} | collective-permute-start | bytes 6152 | tf_op jit(solution)/shard_map/ppermute | solution.py:454
  6.7 11.4 %collective-permute-start.5 = (bf16[256,512]{1,0:T(8,128)(2,1)S(1)}, bf16[256,512]{1,0:T(8,128)(2,1)S(1)}, u32[]{:S(2)}, u32[]{:S(2)}) collective-permute-start(bf16[256,512]{1,0:T(8,128)(2,1)S(1)} %get-tuple-element.9), channel_id=1, source_target_pairs={{0,17},{2,19},{4,21},{6,23},{8,25},{10,27},{12,29},{14,31}} | collective-permute-start | bytes 786440 | tf_op jit(solution)/shard_map/ppermute | solution.py:446
  9.3 12.1 %collective-permute-start.4 = (bf16[256,512]{1,0:T(8,128)(2,1)S(1)}, bf16[256,512]{1,0:T(8,128)(2,1)S(1)}, u32[]{:S(2)}, u32[]{:S(2)}) collective-permute-start(bf16[256,512]{1,0:T(8,128)(2,1)S(1)} %get-tuple-element.9), channel_id=1, source_target_pairs={{0,16},{2,18},{4,20},{6,22},{8,24},{10,26},{12,28},{14,30}} | collective-permute-start | bytes 786440 | tf_op jit(solution)/shard_map/ppermute | solution.py:446
  10.8 34.6 %collective-permute-start.9 = (bf16[128,2048]{1,0:T(8,128)(2,1)}, bf16[128,2048]{1,0:T(8,128)(2,1)S(1)}, u32[]{:S(2)}, u32[]{:S(2)}) collective-permute-start(bf16[128,2048]{1,0:T(8,128)(2,1)} %refs_10_.1), channel_id=1, source_target_pairs={{0,16},{16,0},{1,17},{17,1},{2,18},{18,2},{3,19},{19,3},{4,20},{20... | collective-permute-start | bytes 1572872 | tf_op jit(solution)/shard_map/ppermute | solution.py:461
  11.6 2.6 %collective-permute-start.1 = (s32[1,512]{1,0:T(1,128)S(1)}, s32[1,512]{1,0:T(1,128)S(1)}, u32[]{:S(2)}, u32[]{:S(2)}) collective-permute-start(s32[1,512]{1,0:T(1,128)S(1)} %broadcast_select_fusion), channel_id=1, source_target_pairs={{0,4},{2,6},{1,5},{3,7},{16,20},{18,22},{17,21},{19,23}} | collective-permute-start | bytes 6152 | tf_op jit(solution)/shard_map/ppermute | solution.py:454
  14.2 2.6 %collective-permute-start.2 = (s32[1,512]{1,0:T(1,128)S(1)}, s32[1,512]{1,0:T(1,128)S(1)}, u32[]{:S(2)}, u32[]{:S(2)}) collective-permute-start(s32[1,512]{1,0:T(1,128)S(1)} %broadcast_select_fusion.1.mine_ref), channel_id=1, source_target_pairs={{0,8},{2,10},{4,12},{6,14},{1,9},{3,11},{5,13},{7,15},{16,24},{18,... | collective-permute-start | bytes 6152 | tf_op jit(solution)/shard_map/ppermute | solution.py:454
  15.5 7.2 %collective-permute-start.3 = (bf16[256,512]{1,0:T(8,128)(2,1)S(1)}, bf16[256,512]{1,0:T(8,128)(2,1)S(1)}, u32[]{:S(2)}, u32[]{:S(2)}) collective-permute-start(bf16[256,512]{1,0:T(8,128)(2,1)S(1)} %get-tuple-element.9), channel_id=1, source_target_pairs={{0,1},{2,3},{4,5},{6,7},{8,9},{10,11},{12,13},{14,15}} | collective-permute-start | bytes 786440 | tf_op jit(solution)/shard_map/ppermute | solution.py:446
  16.8 28.6 %collective-permute-start.8 = (bf16[256,512]{1,0:T(8,128)(2,1)S(1)}, bf16[256,512]{1,0:T(8,128)(2,1)S(1)}, u32[]{:S(2)}, u32[]{:S(2)}) collective-permute-start(bf16[256,512]{1,0:T(8,128)(2,1)S(1)} %get-tuple-element.8), channel_id=1, source_target_pairs={{0,17},{2,19},{5,4},{7,6},{24,9},{26,11},{29,28},{31,30}} | collective-permute-start | bytes 786440 | tf_op jit(solution)/shard_map/ppermute | solution.py:446
  18.1 27.2 %collective-permute-start.7 = (bf16[256,512]{1,0:T(8,128)(2,1)S(1)}, bf16[256,512]{1,0:T(8,128)(2,1)S(1)}, u32[]{:S(2)}, u32[]{:S(2)}) collective-permute-start(bf16[256,512]{1,0:T(8,128)(2,1)S(1)} %get-tuple-element.8), channel_id=1, source_target_pairs={{0,16},{2,18},{5,21},{7,23},{24,8},{26,10},{29,13},{31,15}} | collective-permute-start | bytes 786440 | tf_op jit(solution)/shard_map/ppermute | solution.py:446
  21.4 24.0 %collective-permute-start.6 = (bf16[256,512]{1,0:T(8,128)(2,1)S(1)}, bf16[256,512]{1,0:T(8,128)(2,1)S(1)}, u32[]{:S(2)}, u32[]{:S(2)}) collective-permute-start(bf16[256,512]{1,0:T(8,128)(2,1)S(1)} %get-tuple-element.8), channel_id=1, source_target_pairs={{0,1},{2,3},{5,20},{7,22},{24,25},{26,27},{29,12},{31,14}} | collective-permute-start | bytes 786440 | tf_op jit(solution)/shard_map/ppermute | solution.py:446
